TPU v7x, 32 devices: a whole 2x2x4 slice. The times are simulated.
32 devices in a mesh: seq: 8 (over y, x, core), tp: 4 (over z).
Axes of the slice: x: 2, y: 2, z: 4, core: 2. Of those that a mesh axis runs over, the one named last changes fastest.
Arguments:
- grad_out: bfloat16 [1024, 8192], P('seq', 'tp'), may hold values from -6 to 6
- resid_in: bfloat16 [1024, 8192], P('seq', 'tp'), may hold values from -6 to 6
- down_weight: bfloat16 [28672, 8192], P('seq', 'tp'), may hold values from -0.03125 to 0.03125
- hidden_clean: bfloat16 [28672, 512], P('seq', 'tp'), may hold values from -6 to 6
- hidden_corrupt: bfloat16 [28672, 512], P('seq', 'tp'), may hold values from -6 to 6
- patched: int32 [14336], replicated, may hold values from 0 to 28671, as said below
Outputs:
- resid_scores: float32 [1024], P('seq')
- token_scores: float32 [512], P('tp')
- neuron_scores: float32 [28672], P('seq')
Inputs may be any that keep to these rules, and one draw needn't show every extreme that they name: `patched`: 14336 distinct hidden-unit indices.
All inputs are finite; a program needn't handle non-finite values.
Results may differ from a plain program's by a relative error of at most 0.0046.
Values may be sent and summed in bfloat16 or wider, within the bound.
A program may use at most 128 MiB of HBM per device.

v0:
```python
import math
import jax
import jax.numpy as jnp
from jax import lax
from jax.sharding import PartitionSpec as P


def from_behind(value, axis, steps):
    count = lax.axis_size(axis)
    pairs = [(source, (source + steps) % count) for source in range(count)]
    return lax.ppermute(value, axis, pairs)


def patch_mask(patched, unit_rows):
    lanes = math.gcd(unit_rows, 128)
    groups = unit_rows // lanes
    local = patched - lax.axis_index("seq") * unit_rows
    high = local[None, :] // lanes == jnp.arange(groups, dtype=jnp.int32)[:, None]
    high = high & (local >= 0)[None, :]
    low = (local % lanes)[:, None] == jnp.arange(lanes, dtype=jnp.int32)[None, :]
    counts = lax.dot_general(
        high.astype(jnp.bfloat16),
        low.astype(jnp.bfloat16),
        (((1,), (0,)), ((), ())),
        preferred_element_type=jnp.float32,
    )
    return counts.reshape(unit_rows)


def shards(grad_out, resid_in, down_weight, hidden_clean, hidden_corrupt, patched):
    seq_count = lax.axis_size("seq")
    tp_count = lax.axis_size("tp")
    pair_count = seq_count // 2
    half_rows = grad_out.shape[0] // 2
    unit_rows = down_weight.shape[0]
    model_width = resid_in.shape[1] * tp_count
    hidden_diff = (hidden_clean.astype(jnp.float32) - hidden_corrupt.astype(jnp.float32)).astype(
        jnp.bfloat16
    )
    diff_all = lax.all_gather(hidden_diff, "tp", axis=0)
    in_upper = lax.axis_index("seq") // pair_count
    send_start = (1 - in_upper) * half_rows
    keep_start = in_upper * half_rows
    sent_grad = lax.dynamic_slice_in_dim(grad_out, send_start, half_rows, 0)
    partner_grad = from_behind(sent_grad, "seq", pair_count)
    partner_resid = from_behind(resid_in, "seq", pair_count)
    sign_factor = (1 - 2 * in_upper).astype(jnp.float32)
    resid_diff = sign_factor * (resid_in.astype(jnp.float32) - partner_resid.astype(jnp.float32))
    resid_part = jnp.sum(resid_diff * grad_out.astype(jnp.float32), axis=1)
    kept_grad = lax.dynamic_slice_in_dim(grad_out, keep_start, half_rows, 0)
    grad_mean = ((kept_grad.astype(jnp.float32) + partner_grad.astype(jnp.float32)) * 0.5).astype(
        jnp.bfloat16
    )
    grads = lax.all_gather(grad_mean, "seq", axis=0)
    width = grads.shape[-1]
    grads = grads.reshape(2, pair_count, half_rows, width).transpose(1, 0, 2, 3)
    grads = grads.reshape(-1, width)
    total_len = grads.shape[0]
    in_patch = patch_mask(patched, unit_rows)
    unit_grad = lax.dot_general(
        down_weight, grads, (((1,), (1,)), ((), ())), preferred_element_type=jnp.float32
    )
    local_len = total_len // tp_count
    token_parts = []
    unit_part = 0.0
    for block in range(tp_count):
        part = unit_grad[:, block * local_len : (block + 1) * local_len]
        product = diff_all[block].astype(jnp.float32) * part
        token_parts.append(jnp.sum(product * in_patch[:, None], axis=0))
        unit_part = unit_part + jnp.sum(product, axis=1)
    token_part = jnp.stack(token_parts)
    token_total = lax.psum(token_part, ("seq", "tp"))
    token_mine = lax.dynamic_index_in_dim(token_total, lax.axis_index("tp"), 0, keepdims=False)
    token_scores = token_mine / math.sqrt(patched.shape[0])
    unit_total, resid_total = lax.psum((unit_part, resid_part), "tp")
    neuron_scores = unit_total / math.sqrt(total_len)
    resid_scores = resid_total / math.sqrt(model_width)
    return (resid_scores, token_scores, neuron_scores)


def solution(mesh):
    in_specs = (P("seq", "tp"), P("seq", "tp"), P("seq", "tp"), P("seq", "tp"), P("seq", "tp"), P())
    out_specs = (P("seq"), P("tp"), P("seq"))
    return jax.shard_map(shards, mesh=mesh, in_specs=in_specs, out_specs=out_specs, check_vma=False)
```

profile of v0, /device:TPU:10, one launch (start us, length us, event | category | flops | bytes accessed | tf_op | source)
XLA Modules:
  0.0 192.9 jit_solution(12017848095058334556)
XLA Ops:
  7.2 0.0 copy-start.1
  7.2 0.0 copy-start.2
  7.2 0.0 all-gather.7.cloned.1.call-start
  7.3 1.1 constant_dynamic-slice_fusion.1
  8.3 1.6 collective-permute-start.1
  9.9 6.5 %collective-permute-done.1 = bf16[64,2048]{1,0:T(8,128)(2,1)S(1)} collective-permute-done((bf16[64,2048]{1,0:T(8,128)(2,1)S(1)}, bf16[64,2048]{1,0:T(8,128)(2,1)S(1)}, u32[]{:S(2)}, u32[]{:S(2)}) %collective-permute-start.1) | collective-permute-done | bytes 262176 | tf_op jit(solution)/shard_map/ppermute | solution.py:11
  16.5 1.8 multiply_convert_fusion
  18.2 0.0 all-gather.7.cloned.1.call-update
  18.2 0.0 all-gather.5.cloned.1.call-start
  18.3 1.6 collective-permute-start
  19.9 0.0 copy-done.1
  19.9 0.5 copy.14
  20.4 0.0 copy-done.2
  20.4 0.5 copy.13
  20.9 0.0 copy-start.4
  20.9 1.1 subtract_convert_fusion
  22.1 0.0 all-gather.5.cloned.1.call-update
  22.1 0.0 copy-done.4
  22.1 0.1 add_select_fusion.1
  22.2 0.0 copy-start
  22.2 0.0 copy-start.3
  22.2 0.3 fusion.22
  22.6 2.1 %fusion.8 = f32[3584]{0:T(1024)S(1)} fusion(s32[14336]{0:T(1024)S(1)} %get-tuple-element.18, pred[28,14336]{1,0:T(8,128)(4,1)S(1)} %fusion.22), kind=kOutput, calls=%fused_computation.19 | convolution fusion | flops 104595456 | bytes 473088 | tf_op jit(solution)/shard_map/dot_general | solution.py:21
  24.7 9.5 %collective-permute-done = bf16[128,2048]{1,0:T(8,128)(2,1)S(1)} collective-permute-done((bf16[128,2048]{1,0:T(8,128)(2,1)}, bf16[128,2048]{1,0:T(8,128)(2,1)S(1)}, u32[]{:S(2)}, u32[]{:S(2)}) %collective-permute-start) | collective-permute-done | bytes 524320 | tf_op jit(solution)/shard_map/ppermute | solution.py:11
  34.2 0.0 copy-done
  34.2 0.0 copy-done.3
  34.2 0.3 multiply_reduce_fusion.4
  34.5 14.7 %all-gather.7.cloned.1.call-done = bf16[512,2048]{1,0:T(8,128)(2,1)} async-done(((bf16[64,2048]{1,0:T(8,128)(2,1)}), bf16[512,2048]{1,0:T(8,128)(2,1)}) %all-gather.7.cloned.1.call-update) | async-done | bytes 2097168 | tf_op jit(solution)/shard_map/all_gather | solution.py:54
  49.2 1.7 copy.15
  51.0 13.1 %convolution_bitcast_fusion = f32[3584,512]{0,1:T(8,128)} fusion(bf16[512,2048]{1,0:T(8,128)(2,1)S(1)} %bitcast.20, bf16[3584,2048]{1,0:T(8,128)(2,1)} %param.8), kind=kOutput, calls=%fused_computation.2 | convolution fusion | flops 7516192768 | bytes 24117248 | tf_op jit(solution)/shard_map/dot_general | solution.py:60
  64.1 56.5 %all-gather.5.cloned.1.call-done = bf16[14336,128]{0,1:T(8,128)(2,1)} async-done(((bf16[3584,128]{0,1:T(8,128)(2,1)}), bf16[14336,128]{0,1:T(8,128)(2,1)}) %all-gather.5.cloned.1.call-update) | async-done | bytes 3670032 | tf_op jit(solution)/shard_map/all_gather | solution.py:40
  120.5 4.9 %fusion.5 = (f32[3584]{0:T(1024)S(1)}, f32[3584]{0:T(1024)S(1)}, f32[3584]{0:T(1024)S(1)}, f32[3584]{0:T(1024)S(1)}, f32[128]{0:T(128)S(1)}, /*index=5*/f32[128]{0:T(128)S(1)}, f32[128]{0:T(128)S(1)}, f32[128]{0:T(128)S(1)}) fusion(f32[3584,512]{0,1:T(8,128)} %convolution_bitcast_fusion, bf16[14336,128]{0,1:T(8,128)(2,1)} %all-gather.5.cloned.1.call-done, ...), kind=kLoop, calls=%fused_computation.16 | loop fusion | flops 9160192 | bytes 11083776 | tf_op jit(solution)/shard_map/reduce_sum | solution.py:70
  125.4 16.7 %all-reduce = (f32[128]{0:T(128)S(1)}, f32[3584]{0:T(1024)S(1)}) all-reduce(f32[128]{0:T(128)S(1)} %multiply_reduce_fusion.4, f32[3584]{0:T(1024)S(1)} %add_add_fusion), channel_id=1, replica_groups=mesh['seq'=8,'tp'=4] {'tp'}, use_global_device_ids=true, to_apply=%region_1.2 | all-reduce | flops 3712 | bytes 29696 | tf_op jit(solution)/shard_map/psum | solution.py:75
  142.1 0.5 broadcast_multiply_fusion.1
  142.7 42.3 %psum.22 = f32[4,128]{1,0:T(4,128)S(1)} all-reduce(f32[4,128]{1,0:T(4,128)S(1)} %pad_maximum_fusion), channel_id=1, replica_groups=mesh['seq'=8,'tp'=4] {'seq','tp'}, use_global_device_ids=true, to_apply=%region_6.7 | all-reduce | flops 512 | bytes 4096 | tf_op jit(solution)/shard_map/psum | solution.py:72
  185.0 0.6 broadcast_multiply_fusion
  185.6 0.5 fusion.16
  (3 shorter events, 0.0 us)
Async XLA Ops:
  7.2 12.7 %copy-start.1 = (bf16[3584,128]{1,0:T(8,128)(2,1)S(1)}, bf16[3584,128]{1,0:T(8,128)(2,1)}, u32[]{:S(2)}) copy-start(bf16[3584,128]{1,0:T(8,128)(2,1)} %param.10) | copy-start | bytes 2752516
  7.2 13.2 %copy-start.2 = (bf16[3584,128]{1,0:T(8,128)(2,1)S(1)}, bf16[3584,128]{1,0:T(8,128)(2,1)}, u32[]{:S(2)}) copy-start(bf16[3584,128]{1,0:T(8,128)(2,1)} %param.9) | copy-start | bytes 2752516
  7.2 42.0 %all-gather.7.cloned.1.call-start = ((), (), s32[]{:S(2)}) async-start(), calls=%async_computation.1 | async-start | bytes 2359296 | tf_op jit(solution)/shard_map/all_gather | solution.py:54
  8.3 8.1 %collective-permute-start.1 = (bf16[64,2048]{1,0:T(8,128)(2,1)S(1)}, bf16[64,2048]{1,0:T(8,128)(2,1)S(1)}, u32[]{:S(2)}, u32[]{:S(2)}) collective-permute-start(bf16[64,2048]{1,0:T(8,128)(2,1)S(1)} %constant_dynamic-slice_fusion.1), channel_id=1, source_target_pairs={{0,16},{4,20},{8,24},{12,28},{16,0},{20,4},{24,8},{28,12},{1,17},{... | collective-permute-start | bytes 786440 | tf_op jit(solution)/shard_map/ppermute | solution.py:11
  18.2 102.3 %all-gather.5.cloned.1.call-start = ((), (), s32[]{:S(2)}) async-start(), calls=%async_computation | async-start | bytes 4587520 | tf_op jit(solution)/shard_map/all_gather | solution.py:40
  18.3 15.9 %collective-permute-start = (bf16[128,2048]{1,0:T(8,128)(2,1)}, bf16[128,2048]{1,0:T(8,128)(2,1)S(1)}, u32[]{:S(2)}, u32[]{:S(2)}) collective-permute-start(bf16[128,2048]{1,0:T(8,128)(2,1)} %param.7), channel_id=1, source_target_pairs={{0,16},{4,20},{8,24},{12,28},{16,0},{20,4},{24,8},{28,12},{1,17},{... | collective-permute-start | bytes 1572872 | tf_op jit(solution)/shard_map/ppermute | solution.py:11
  20.9 1.2 copy-start.4
  22.2 12.0 %copy-start = (bf16[128,2048]{1,0:T(8,128)(2,1)S(1)}, bf16[128,2048]{1,0:T(8,128)(2,1)}, u32[]{:S(2)}) copy-start(bf16[128,2048]{1,0:T(8,128)(2,1)} %param.6) | copy-start | bytes 1572868
  22.2 11.9 %copy-start.3 = (bf16[128,2048]{1,0:T(8,128)(2,1)S(1)}, bf16[128,2048]{1,0:T(8,128)(2,1)}, u32[]{:S(2)}) copy-start(bf16[128,2048]{1,0:T(8,128)(2,1)} %param.7) | copy-start | bytes 1572868
Sparse Core Ops, SparseCore 0:
  18.4 30.8 all-gather.6
  50.8 69.7 all-gather.4
where the time goes:
time: 193 us
  waiting for transfers between devices  87.2 us (45%)
  blocking collectives  59 us (31%)
  matrix products  15.2 us (8%)
  between operations  14.2 us (7%)
  other arithmetic  10.2 us (5%)
  local copies, waits for them, and re-layouts  3.87 us (2%)
  starting transfers between devices  3.25 us (2%)
    all_gather x1, waiting for transfers between devices, shards(): diff_all = lax.all_gather(hidden_diff, 'tp', axis=0)  56.5 us
    psum x1, blocking collectives, shards(): token_total = lax.psum(token_part, ('seq', 'tp'))  42.3 us
    psum x1, blocking collectives, shards(): unit_total, resid_total = lax.psum((unit_part, resid_part), 'tp')  16.7 us
    ppermute x2, waiting for transfers between devices, from_behind(): return lax.ppermute(value, axis, pairs)  16 us
    all_gather x1, waiting for transfers between devices, shards(): grads = lax.all_gather(grad_mean, 'seq', axis=0)  14.7 us
    dot_general x1, matrix products, shards(): lax.dot_general(down_weight, grads, (((1,), (1,)), ((), ())), preferred_e...  13.1 us
    reduce_sum x1, other arithmetic, shards(): unit_part = unit_part + jnp.sum(product, axis=1)  4.87 us
  transfers between devices with their start and end apart: 4, of which 4 were waited for; matrix products, arithmetic and copies ran while one was open for 10% of the time, Pallas kernels for 0%

commit v1 on v0

--- a/solution.py
+++ b/solution.py
@@ -3,6 +3,11 @@
 import jax.numpy as jnp
 from jax import lax
 from jax.sharding import PartitionSpec as P
+from jax.lax import all_gather
+
+
+def part_the_skins(mesh_dim, base_x):
+    return jnp.sum(all_gather(base_x, mesh_dim), 0)
 
 
 def from_behind(value, axis, steps):
@@ -69,7 +74,7 @@
         token_parts.append(jnp.sum(product * in_patch[:, None], axis=0))
         unit_part = unit_part + jnp.sum(product, axis=1)
     token_part = jnp.stack(token_parts)
-    token_total = lax.psum(token_part, ("seq", "tp"))
+    token_total = part_the_skins(("seq", "tp"), token_part)
     token_mine = lax.dynamic_index_in_dim(token_total, lax.axis_index("tp"), 0, keepdims=False)
     token_scores = token_mine / math.sqrt(patched.shape[0])
     unit_total, resid_total = lax.psum((unit_part, resid_part), "tp")

time: 193 us -> 218 us (1.13)
  the two profiles are of different devices: /device:TPU:10 before, /device:TPU:0 now
where the time goes in v1:
time: 218 us
  waiting for transfers between devices  89.5 us (41%)
  blocking collectives  80.1 us (37%)
  matrix products  15.2 us (7%)
  between operations  14.2 us (7%)
  other arithmetic  10.2 us (5%)
  starting transfers between devices  4.92 us (2%)
  local copies, waits for them, and re-layouts  3.87 us (2%)
    all_gather x1, blocking collectives, part_the_skins(): return jnp.sum(all_gather(base_x, mesh_dim), 0)  63.8 us
    all_gather x1, waiting for transfers between devices, shards(): diff_all = lax.all_gather(hidden_diff, 'tp', axis=0)  58.9 us
    psum x1, blocking collectives, shards(): unit_total, resid_total = lax.psum((unit_part, resid_part), 'tp')  16.2 us
    ppermute x2, waiting for transfers between devices, from_behind(): return lax.ppermute(value, axis, pairs)  15.9 us
    all_gather x1, waiting for transfers between devices, shards(): grads = lax.all_gather(grad_mean, 'seq', axis=0)  14.7 us
    dot_general x1, matrix products, shards(): lax.dot_general(down_weight, grads, (((1,), (1,)), ((), ())), preferred_e...  13.1 us
    reduce_sum x1, other arithmetic, shards(): unit_part = unit_part + jnp.sum(product, axis=1)  4.87 us
    ppermute x2, starting transfers between devices, from_behind(): return lax.ppermute(value, axis, pairs)  4.84 us
  transfers between devices with their start and end apart: 4, of which 4 were waited for; matrix products, arithmetic and copies ran while one was open for 9% of the time, Pallas kernels for 0%

profile of v1, /device:TPU:0, one launch (start us, length us, event | category | flops | bytes accessed | tf_op | source)
XLA Modules:
  0.0 218.0 jit_solution(11252999971586606990)
XLA Ops:
  7.2 0.0 copy-start.1
  7.2 0.0 copy-start.2
  7.2 0.0 all-gather.9.cloned.1.call-start
  7.3 1.1 constant_dynamic-slice_fusion.1
  8.3 3.0 %collective-permute-start.1 = (bf16[64,2048]{1,0:T(8,128)(2,1)S(1)}, bf16[64,2048]{1,0:T(8,128)(2,1)S(1)}, u32[]{:S(2)}, u32[]{:S(2)}) collective-permute-start(bf16[64,2048]{1,0:T(8,128)(2,1)S(1)} %constant_dynamic-slice_fusion.1), channel_id=1, source_target_pairs={{0,16},{4,20},{8,24},{12,28},{16,0},{20,4},{24,8},{28,12},{1,17},{... | collective-permute-start | bytes 786440 | tf_op jit(solution)/shard_map/ppermute | solution.py:16
  11.4 6.3 %collective-permute-done.1 = bf16[64,2048]{1,0:T(8,128)(2,1)S(1)} collective-permute-done((bf16[64,2048]{1,0:T(8,128)(2,1)S(1)}, bf16[64,2048]{1,0:T(8,128)(2,1)S(1)}, u32[]{:S(2)}, u32[]{:S(2)}) %collective-permute-start.1) | collective-permute-done | bytes 262176 | tf_op jit(solution)/shard_map/ppermute | solution.py:16
  17.7 1.8 multiply_convert_fusion
  19.4 0.0 all-gather.9.cloned.1.call-update
  19.5 0.0 all-gather.7.cloned.1.call-start
  19.5 1.8 collective-permute-start
  21.3 0.0 copy-done.1
  21.3 0.5 copy.17
  21.8 0.0 copy-done.2
  21.9 0.5 copy.16
  22.4 0.0 copy-start.4
  22.4 1.1 subtract_convert_fusion
  23.5 0.0 all-gather.7.cloned.1.call-update
  23.6 0.0 copy-done.4
  23.6 0.1 add_select_fusion.1
  23.7 0.0 copy-start
  23.7 0.0 copy-start.3
  23.7 0.3 fusion.22
  24.0 2.1 fusion.8
  26.1 9.6 %collective-permute-done = bf16[128,2048]{1,0:T(8,128)(2,1)S(1)} collective-permute-done((bf16[128,2048]{1,0:T(8,128)(2,1)}, bf16[128,2048]{1,0:T(8,128)(2,1)S(1)}, u32[]{:S(2)}, u32[]{:S(2)}) %collective-permute-start) | collective-permute-done | bytes 524320 | tf_op jit(solution)/shard_map/ppermute | solution.py:16
  35.7 0.0 copy-done
  35.7 0.0 copy-done.3
  35.7 0.4 multiply_reduce_fusion.4
  36.1 14.7 %all-gather.9.cloned.1.call-done = bf16[512,2048]{1,0:T(8,128)(2,1)} async-done(((bf16[64,2048]{1,0:T(8,128)(2,1)}), bf16[512,2048]{1,0:T(8,128)(2,1)}) %all-gather.9.cloned.1.call-update) | async-done | bytes 2097168 | tf_op jit(solution)/shard_map/all_gather | solution.py:59
  50.8 1.7 copy.18
  52.5 13.1 %convolution_bitcast_fusion = f32[3584,512]{0,1:T(8,128)} fusion(bf16[512,2048]{1,0:T(8,128)(2,1)S(1)} %bitcast.22, bf16[3584,2048]{1,0:T(8,128)(2,1)} %param.8), kind=kOutput, calls=%fused_computation.2 | convolution fusion | flops 7516192768 | bytes 24117248 | tf_op jit(solution)/shard_map/dot_general | solution.py:65
  65.6 58.9 %all-gather.7.cloned.1.call-done = bf16[14336,128]{0,1:T(8,128)(2,1)} async-done(((bf16[3584,128]{0,1:T(8,128)(2,1)}), bf16[14336,128]{0,1:T(8,128)(2,1)}) %all-gather.7.cloned.1.call-update) | async-done | bytes 3670032 | tf_op jit(solution)/shard_map/all_gather | solution.py:45
  124.5 4.9 %fusion.5 = (f32[3584]{0:T(1024)S(1)}, f32[3584]{0:T(1024)S(1)}, f32[3584]{0:T(1024)S(1)}, f32[3584]{0:T(1024)S(1)}, f32[128]{0:T(128)S(1)}, /*index=5*/f32[128]{0:T(128)S(1)}, f32[128]{0:T(128)S(1)}, f32[128]{0:T(128)S(1)}) fusion(f32[3584,512]{0,1:T(8,128)} %convolution_bitcast_fusion, bf16[14336,128]{0,1:T(8,128)(2,1)} %all-gather.7.cloned.1.call-done, ...), kind=kLoop, calls=%fused_computation.16 | loop fusion | flops 9160192 | bytes 11083776 | tf_op jit(solution)/shard_map/reduce_sum | solution.py:75
  129.4 16.2 %all-reduce = (f32[128]{0:T(128)S(1)}, f32[3584]{0:T(1024)S(1)}) all-reduce(f32[128]{0:T(128)S(1)} %multiply_reduce_fusion.4, f32[3584]{0:T(1024)S(1)} %add_add_fusion), channel_id=1, replica_groups=mesh['seq'=8,'tp'=4] {'tp'}, use_global_device_ids=true, to_apply=%region_1.2 | all-reduce | flops 3712 | bytes 29696 | tf_op jit(solution)/shard_map/psum | solution.py:80
  145.6 0.5 broadcast_multiply_fusion.1
  146.2 63.8 %all-gather.3 = f32[32,4,128]{2,1,0:T(4,128)S(1)} all-gather(f32[1,4,128]{2,1,0:T(4,128)S(1)} %maximum_bitcast_fusion), channel_id=4, replica_groups=mesh['seq'=8,'tp'=4] {'seq','tp'}, dimensions={0}, use_global_device_ids=true | all-gather | bytes 67584 | tf_op jit(solution)/shard_map/all_gather | solution.py:10
  210.0 0.6 broadcast_multiply_fusion
  210.6 0.5 fusion.16
  (4 shorter events, 0.1 us)
Async XLA Ops:
  7.2 14.2 %copy-start.1 = (bf16[3584,128]{1,0:T(8,128)(2,1)S(1)}, bf16[3584,128]{1,0:T(8,128)(2,1)}, u32[]{:S(2)}) copy-start(bf16[3584,128]{1,0:T(8,128)(2,1)} %param.10) | copy-start | bytes 2752516
  7.2 14.7 %copy-start.2 = (bf16[3584,128]{1,0:T(8,128)(2,1)S(1)}, bf16[3584,128]{1,0:T(8,128)(2,1)}, u32[]{:S(2)}) copy-start(bf16[3584,128]{1,0:T(8,128)(2,1)} %param.9) | copy-start | bytes 2752516
  7.2 43.6 %all-gather.9.cloned.1.call-start = ((), (), s32[]{:S(2)}) async-start(), calls=%async_computation.1 | async-start | bytes 2359296 | tf_op jit(solution)/shard_map/all_gather | solution.py:59
  8.3 9.3 %collective-permute-start.1 = (bf16[64,2048]{1,0:T(8,128)(2,1)S(1)}, bf16[64,2048]{1,0:T(8,128)(2,1)S(1)}, u32[]{:S(2)}, u32[]{:S(2)}) collective-permute-start(bf16[64,2048]{1,0:T(8,128)(2,1)S(1)} %constant_dynamic-slice_fusion.1), channel_id=1, source_target_pairs={{0,16},{4,20},{8,24},{12,28},{16,0},{20,4},{24,8},{28,12},{1,17},{... | collective-permute-start | bytes 786440 | tf_op jit(solution)/shard_map/ppermute | solution.py:16
  19.5 105.0 %all-gather.7.cloned.1.call-start = ((), (), s32[]{:S(2)}) async-start(), calls=%async_computation | async-start | bytes 4587520 | tf_op jit(solution)/shard_map/all_gather | solution.py:45
  19.5 16.2 %collective-permute-start = (bf16[128,2048]{1,0:T(8,128)(2,1)}, bf16[128,2048]{1,0:T(8,128)(2,1)S(1)}, u32[]{:S(2)}, u32[]{:S(2)}) collective-permute-start(bf16[128,2048]{1,0:T(8,128)(2,1)} %param.7), channel_id=1, source_target_pairs={{0,16},{4,20},{8,24},{12,28},{16,0},{20,4},{24,8},{28,12},{1,17},{... | collective-permute-start | bytes 1572872 | tf_op jit(solution)/shard_map/ppermute | solution.py:16
  22.4 1.2 copy-start.4
  23.7 12.1 %copy-start = (bf16[128,2048]{1,0:T(8,128)(2,1)S(1)}, bf16[128,2048]{1,0:T(8,128)(2,1)}, u32[]{:S(2)}) copy-start(bf16[128,2048]{1,0:T(8,128)(2,1)} %param.6) | copy-start | bytes 1572868
  23.7 12.0 %copy-start.3 = (bf16[128,2048]{1,0:T(8,128)(2,1)S(1)}, bf16[128,2048]{1,0:T(8,128)(2,1)}, u32[]{:S(2)}) copy-start(bf16[128,2048]{1,0:T(8,128)(2,1)} %param.7) | copy-start | bytes 1572868
Sparse Core Ops, SparseCore 0:
  19.6 31.1 all-gather.8
  52.4 72.1 all-gather.6
